TPU v7x, 32 devices: a whole 2x2x4 slice. The times are simulated.
32 devices in a mesh: fsdp: 8 (over z, y), ctx: 2 (over x), tp: 2 (over core).
Axes of the slice: x: 2, y: 2, z: 4, core: 2. Of those that a mesh axis runs over, the one named last changes fastest.
Arguments:
- tokens: bfloat16 [3584, 2304], P(('fsdp', 'ctx')), may hold values from -6 to 6
- cotangent: bfloat16 [3584, 2304], P(('fsdp', 'ctx')), may hold values from -6 to 6
- lengths: int32 [8, 1], P('fsdp'), may hold values from 224 to 448, as said below
- positions: int32 [8, 448], P('fsdp'), may hold values from 0 to 447, each once within a row
- query_weight: bfloat16 [2304, 2048], P('fsdp', 'tp'), may hold values from -0.5 to 0.5
- key_weight: bfloat16 [2304, 1024], P('fsdp', 'tp'), may hold values from -0.5 to 0.5
- value_weight: bfloat16 [2304, 1024], P('fsdp', 'tp'), may hold values from -0.125 to 0.125
- output_weight: bfloat16 [2048, 2304], P('tp', 'fsdp'), may hold values from -0.125 to 0.125
- gate_weight: bfloat16 [2304, 9216], P('fsdp', 'tp'), may hold values from -0.125 to 0.125
- up_weight: bfloat16 [2304, 9216], P('fsdp', 'tp'), may hold values from -0.125 to 0.125
- down_weight: bfloat16 [9216, 2304], P('tp', 'fsdp'), may hold values from -0.0625 to 0.0625
- gain_attn_in: bfloat16 [2304], P('fsdp'), may hold values from -0.5 to 0.5
- gain_attn_out: bfloat16 [2304], P('fsdp'), may hold values from -0.5 to 0.5
- gain_ffn_in: bfloat16 [2304], P('fsdp'), may hold values from -0.5 to 0.5
- gain_ffn_out: bfloat16 [2304], P('fsdp'), may hold values from -0.5 to 0.5
Outputs:
- block_out: bfloat16 [3584, 2304], P(('fsdp', 'ctx'))
- tokens_grad: bfloat16 [3584, 2304], P(('fsdp', 'ctx'))
- query_weight_grad: float32 [2304, 2048], P(('fsdp', 'ctx'), 'tp')
- key_weight_grad: float32 [2304, 1024], P(('fsdp', 'ctx'), 'tp')
- value_weight_grad: float32 [2304, 1024], P(('fsdp', 'ctx'), 'tp')
- output_weight_grad: float32 [2048, 2304], P('tp', ('fsdp', 'ctx'))
- gate_weight_grad: float32 [2304, 9216], P(('fsdp', 'ctx'), 'tp')
- up_weight_grad: float32 [2304, 9216], P(('fsdp', 'ctx'), 'tp')
- down_weight_grad: float32 [9216, 2304], P('tp', ('fsdp', 'ctx'))
- gain_attn_in_grad: float32 [2304], P(('fsdp', 'ctx'))
- gain_attn_out_grad: float32 [2304], P(('fsdp', 'ctx'))
- gain_ffn_in_grad: float32 [2304], P(('fsdp', 'ctx'))
- gain_ffn_out_grad: float32 [2304], P(('fsdp', 'ctx'))
Inputs may be any that keep to these rules, and one draw needn't show every extreme that they name: lengths[g, 0] is the number of live tokens of group g's sequence; in every draw some group has exactly 448 and another exactly 224. Each row of positions is a permutation of 0 to 447.
All inputs are finite; a program needn't handle non-finite values.
Results may differ from a plain program's by a relative error of at most 0.018.
The roundings to bfloat16 on the way count: a program that leaves them out, or rounds other values in their place, can miss the bound.
Values may be sent and summed in bfloat16 or wider, within the bound.
No kernel may reach another device: no remote copies, remote signals or barrier semaphores. Data moves between devices by JAX's collectives and lax.ppermute only.
A program may use at most 640 MiB of HBM per device.

v0:
```python
import functools
import jax
import jax.numpy as jnp
from jax import lax
from jax.sharding import PartitionSpec as P

HEAD_DIM = 256
eps_norm = 1e-06
soft_cap = 50.0
f32 = jnp.float32
b16 = jnp.bfloat16


def rms_scale(field, gain_vec):
    factor = lax.rsqrt(jnp.mean(field * field, axis=-1, keepdims=True) + eps_norm)
    return field * factor * (1.0 + gain_vec)


def gelu_tanh(value_in):
    return (
        0.5
        * value_in
        * (
            1.0
            + jnp.tanh(0.7978845608028654 * (value_in + 0.044715 * value_in * value_in * value_in))
        )
    )


def glu_apply(gate_act, up_act):
    return gelu_tanh(gate_act) * up_act


def norm_back(field, gain_vec, cot_in):
    pullback = jax.vjp(rms_scale, field, gain_vec)[1]
    return pullback(cot_in)


def placement_of(doc_lengths, packed):
    doc_ends = jnp.cumsum(doc_lengths)
    after_end = packed[:, None] >= doc_ends[None, :]
    segment = jnp.sum(after_end.astype(jnp.int32), axis=1)
    inner = packed - jnp.sum(jnp.where(after_end, doc_lengths[None, :], 0), axis=1)
    return (segment, inner)


def angles_of(inner, head_size):
    half_size = head_size // 2
    freq = jnp.power(10000.0, -jnp.arange(half_size, dtype=f32) * (2.0 / head_size))
    return inner.astype(f32)[:, None] * freq[None, :]


def rotate(field, angles):
    half_size = field.shape[-1] // 2
    cosine = jnp.cos(angles)[:, None, :]
    sine = jnp.sin(angles)[:, None, :]
    first_half = field[..., :half_size]
    second_half = field[..., half_size:]
    return jnp.concatenate(
        [first_half * cosine - second_half * sine, second_half * cosine + first_half * sine],
        axis=-1,
    )


def dot(lhs, rhs, dims):
    return lax.dot_general(lhs, rhs, (dims, ((), ())), preferred_element_type=f32)


def swap(piece, axis):
    return lax.ppermute(piece, axis, [(0, 1), (1, 0)])


def hop(piece, step, n):
    return lax.ppermute(piece, "fsdp", [(d, d ^ step) for d in range(n)])


def gather_rows(own, n):
    have = [own]
    bit = n // 2
    while bit:
        have = have + [hop(piece, bit, n) for piece in have]
        bit //= 2
    mine = jnp.concatenate(have)
    return jnp.concatenate([mine, swap(mine, "tp")])


def scatter_rows(part, n):
    rows = part.shape[0] // (2 * n)
    most = n * rows
    both = part[:most] + swap(part[most:].astype(b16), "tp").astype(f32)
    blocks = [both[k * rows : (k + 1) * rows] for k in range(n)]
    bit = 1
    while bit < n:
        keep = len(blocks) // 2
        blocks = [
            blocks[k] + hop(blocks[keep + k].astype(b16), bit, n).astype(f32) for k in range(keep)
        ]
        bit *= 2
    return blocks[0]


def gather_group(own):
    across = swap(own, "ctx")
    beside = swap(jnp.concatenate([own, across]), "tp")
    rows = own.shape[0]
    return jnp.concatenate([own, beside[:rows], across, beside[rows:]])


def scatter_group(part):
    rows = part.shape[0] // 4
    b0, b1, b2, b3 = [part[k * rows : (k + 1) * rows] for k in range(4)]
    got = swap(jnp.concatenate([b1, b3]), "tp")
    return b0 + got[:rows] + swap(b2 + got[rows:], "ctx")


def natural(own, other, index, axis):
    first = jnp.where(index == 0, own, other)
    second = jnp.where(index == 0, other, own)
    return jnp.concatenate([first, second], axis=axis)


def local(
    n,
    tokens,
    cotangent,
    lengths,
    positions,
    query_weight,
    key_weight,
    value_weight,
    output_weight,
    gate_weight,
    up_weight,
    down_weight,
    gain_attn_in,
    gain_attn_out,
    gain_ffn_in,
    gain_ffn_out,
):
    me = lax.axis_index("fsdp")
    ctx = lax.axis_index("ctx")
    tp = lax.axis_index("tp")
    tok_rows, width = tokens.shape
    rows = tok_rows // 2
    head_size = HEAD_DIM
    d_rows = query_weight.shape[0]
    d_half = d_rows // 2
    q_cols = query_weight.shape[1] // 2
    k_cols = key_weight.shape[1] // 2
    q_local = q_cols // head_size
    kv_local = k_cols // head_size
    group_size = q_local // kv_local
    query_scale = head_size ** (-0.5)
    ff_local = gate_weight.shape[1]
    ff_own = ff_local // n
    starts = [c * tok_rows + t * rows for c in (ctx, 1 - ctx) for t in (tp, 1 - tp)]
    packed = jnp.concatenate(
        [lax.dynamic_slice_in_dim(positions[0], start, rows) for start in starts]
    )
    segment, inner = placement_of(lengths[0], packed)
    angles = angles_of(inner, head_size)
    allowed = (segment[:, None] == segment[None, :]) & (inner[None, :] <= inner[:, None])
    mine = lax.dynamic_slice_in_dim(tokens, tp * rows, rows)
    across = swap(mine, "ctx")
    beside = swap(across, "tp")
    seq_group = jnp.concatenate([tokens, across, beside])
    row_ids = jnp.arange(rows, dtype=jnp.int32)
    seq_ids = jnp.concatenate(
        [
            ctx * tok_rows + jnp.arange(tok_rows, dtype=jnp.int32),
            starts[2] + row_ids,
            starts[3] + row_ids,
        ]
    )
    pick = (packed[:, None] == seq_ids[None, :]).astype(b16)
    slot_in = dot(pick, seq_group, ((1,), (0,)))
    resid_in = slot_in[:rows]
    qkv_own = jnp.concatenate(
        [
            lax.dynamic_slice_in_dim(query_weight, ctx * q_cols, q_cols, 1),
            lax.dynamic_slice_in_dim(key_weight, ctx * k_cols, k_cols, 1),
            lax.dynamic_slice_in_dim(value_weight, ctx * k_cols, k_cols, 1),
        ],
        axis=1,
    )
    qkv_weight = lax.all_gather(qkv_own, "fsdp", axis=0, tiled=True)
    out_own = lax.dynamic_slice_in_dim(output_weight, ctx * q_cols, q_cols, 0).T
    out_weight = lax.all_gather(out_own, "fsdp", axis=0, tiled=True)
    gains = lax.all_gather(
        jnp.concatenate([gain_attn_in, gain_attn_out, gain_ffn_in, gain_ffn_out])
        .astype(f32)
        .reshape(1, 4 * d_rows),
        "fsdp",
        axis=0,
        tiled=True,
    )
    gains = gains.reshape(n, 4, d_rows).transpose(1, 0, 2).reshape(4, width)
    ffn_own = jnp.stack([gate_weight, up_weight, down_weight.T])
    ffn_own = ffn_own.reshape(3, 2, d_half, n, ff_own).transpose(3, 1, 0, 2, 4)
    ffn_own = lax.dynamic_index_in_dim(ffn_own, ctx, 1, keepdims=False)
    ffn_full = [jnp.zeros((n, 2, d_half, ff_own), b16) for _ in range(3)]
    for k in range(n):
        piece = lax.dynamic_index_in_dim(ffn_own, me ^ k, 0, keepdims=False)
        if k:
            piece = hop(piece, k, n)
        second = swap(piece, "ctx")
        for which in range(3):
            for half, side in ((piece, ctx), (second, 1 - ctx)):
                ffn_full[which] = lax.dynamic_update_slice(
                    ffn_full[which], half[which][None, None], (me ^ k, side, 0, 0)
                )
    gate_full, up_full, down_full = [full.reshape(width, ff_own) for full in ffn_full]
    normed_attn = rms_scale(slot_in, gains[0]).astype(b16)
    qkv = dot(normed_attn, qkv_weight, ((1,), (0,)))
    all_rows = 2 * tok_rows
    query_lin = qkv[:, :q_cols].reshape(all_rows, q_local, head_size)
    key_lin = qkv[:, q_cols : q_cols + k_cols].reshape(all_rows, kv_local, head_size)
    values = qkv[:, q_cols + k_cols :].astype(b16).reshape(all_rows, kv_local, head_size)
    queries = (rotate(query_lin, angles) * query_scale).astype(b16)
    queries = queries.reshape(all_rows, kv_local, group_size, head_size)
    keys = rotate(key_lin, angles).astype(b16)
    raw_scores = jnp.einsum("qkgd,skd->kgqs", queries, keys, preferred_element_type=f32)
    tanh_ratio = jnp.tanh(raw_scores / soft_cap)
    masked = jnp.where(allowed[None, None], soft_cap * tanh_ratio, -1e30)
    row_peak = jnp.max(masked, axis=-1, keepdims=True)
    exp_terms = jnp.exp(masked - row_peak)
    probs = exp_terms / jnp.sum(exp_terms, axis=-1, keepdims=True)
    probs_low = probs.astype(b16)
    attended = (
        jnp.einsum("kgqs,skd->qkgd", probs_low, values, preferred_element_type=f32)
        .reshape(all_rows, q_cols)
        .astype(b16)
    )
    attn_out = scatter_group(dot(attended, out_weight, ((1,), (1,))))
    middle = resid_in + rms_scale(attn_out, gains[1])
    normed_ffn = gather_rows(rms_scale(middle, gains[2]).astype(b16), n)
    gate_act = dot(normed_ffn, gate_full, ((1,), (0,)))
    up_act = dot(normed_ffn, up_full, ((1,), (0,)))
    hidden = glu_apply(gate_act, up_act).astype(b16)
    ffn_out = scatter_rows(dot(hidden, down_full, ((1,), (1,))), n)
    block_own = (middle + rms_scale(ffn_out, gains[3])).astype(b16)
    block_out = natural(block_own, swap(block_own, "tp"), tp, 0)
    d_out = lax.dynamic_slice_in_dim(cotangent, tp * rows, rows).astype(f32)
    d_ffn_raw, gain_four_term = norm_back(ffn_out, gains[3], d_out)
    d_ffn_out = gather_rows(d_ffn_raw.astype(b16), n)
    d_hidden = dot(d_ffn_out, down_full, ((1,), (0,)))
    d_gate_raw, d_up_raw = jax.vjp(glu_apply, gate_act, up_act)[1](d_hidden)
    d_gate = d_gate_raw.astype(b16)
    d_up = d_up_raw.astype(b16)
    d_normed_ffn = scatter_rows(
        dot(d_gate, gate_full, ((1,), (1,))) + dot(d_up, up_full, ((1,), (1,))), n
    )
    ffn_terms = [
        dot(normed_ffn, d_gate, ((0,), (0,))),
        dot(normed_ffn, d_up, ((0,), (0,))),
        dot(d_ffn_out, hidden, ((0,), (0,))),
    ]
    ffn_terms = [term.reshape(n, 2, d_half, ff_own) for term in ffn_terms]
    ffn_keep = [lax.dynamic_index_in_dim(term, ctx, 1, keepdims=False) for term in ffn_terms]
    ffn_send = [
        lax.dynamic_index_in_dim(term, 1 - ctx, 1, keepdims=False).astype(b16) for term in ffn_terms
    ]
    ffn_sum = [keep + swap(send, "ctx").astype(f32) for keep, send in zip(ffn_keep, ffn_send)]
    ffn_low = jnp.stack([term.astype(b16) for term in ffn_sum], axis=1)
    ffn_grads = ffn_sum
    for k in range(1, n):
        piece = hop(lax.dynamic_index_in_dim(ffn_low, me ^ k, 0, keepdims=False), k, n)
        ffn_grads = [
            lax.dynamic_update_index_in_dim(grad, piece[which].astype(f32), me ^ k, 0)
            for which, grad in enumerate(ffn_grads)
        ]
    gate_weight_grad = ffn_grads[0].transpose(1, 0, 2).reshape(d_half, ff_local)
    up_weight_grad = ffn_grads[1].transpose(1, 0, 2).reshape(d_half, ff_local)
    down_weight_grad = ffn_grads[2].transpose(0, 2, 1).reshape(ff_local, d_half)
    d_middle_part, gain_three_term = norm_back(middle, gains[2], d_normed_ffn)
    d_middle = d_out + d_middle_part
    d_attn_raw, gain_two_term = norm_back(attn_out, gains[1], d_middle)
    d_attn_out = gather_group(d_attn_raw.astype(b16))
    d_attended = dot(d_attn_out, out_weight, ((1,), (0,))).astype(b16)
    d_att = d_attended.reshape(all_rows, kv_local, group_size, head_size)
    d_probs = jnp.einsum("qkgd,skd->kgqs", d_att, values, preferred_element_type=f32)
    d_soft = probs * (d_probs - jnp.sum(probs * d_probs, axis=-1, keepdims=True))
    d_scores = (d_soft * (1.0 - tanh_ratio * tanh_ratio)).astype(b16)
    d_queries = jnp.einsum("kgqs,skd->qkgd", d_scores, keys, preferred_element_type=f32)
    d_keys = jnp.einsum("kgqs,qkgd->skd", d_scores, queries, preferred_element_type=f32)
    d_values = jnp.einsum("kgqs,qkgd->skd", probs_low, d_att, preferred_element_type=f32)
    d_query_lin = (
        rotate(d_queries.reshape(all_rows, q_local, head_size) * query_scale, -angles)
        .reshape(all_rows, q_cols)
        .astype(b16)
    )
    d_key_lin = rotate(d_keys, -angles).reshape(all_rows, k_cols).astype(b16)
    d_value = d_values.reshape(all_rows, k_cols).astype(b16)
    d_qkv = jnp.concatenate([d_query_lin, d_key_lin, d_value], axis=1)
    d_normed_attn = scatter_group(dot(d_qkv, qkv_weight, ((1,), (1,))))
    resid_part, gain_one_term = norm_back(resid_in, gains[0], d_normed_attn)
    slot_grad = gather_group((d_middle + resid_part).astype(b16))
    place = (
        (ctx * tok_rows + jnp.arange(tok_rows, dtype=jnp.int32))[:, None] == packed[None, :]
    ).astype(b16)
    tokens_grad = dot(place, slot_grad, ((1,), (0,))).astype(b16)
    attn_terms = jnp.concatenate(
        [dot(normed_attn, d_qkv, ((0,), (0,))), dot(d_attn_out, attended, ((0,), (0,)))], axis=1
    ).astype(b16)
    attn_rows = lax.psum_scatter(attn_terms, "fsdp", scatter_dimension=0, tiled=True)
    attn_rows = attn_rows.reshape(2, d_half, -1)
    attn_own = lax.dynamic_index_in_dim(attn_rows, ctx, 0, keepdims=False)
    attn_other = swap(lax.dynamic_index_in_dim(attn_rows, 1 - ctx, 0, keepdims=False), "ctx")
    edges = [0, q_cols, q_cols + k_cols, q_cols + 2 * k_cols, 2 * q_cols + 2 * k_cols]
    attn_grads = [
        natural(attn_own[:, a:b].astype(f32), attn_other[:, a:b].astype(f32), ctx, 1)
        for a, b in zip(edges[:-1], edges[1:])
    ]
    gain_terms = jnp.stack([gain_one_term, gain_two_term, gain_three_term, gain_four_term])
    gain_terms = gain_terms.reshape(4, 2 * n, d_half).transpose(1, 0, 2).reshape(2 * n, 4 * d_half)
    gain_terms = gain_terms + swap(gain_terms, "tp")
    gain_rows = lax.psum_scatter(gain_terms, ("fsdp", "ctx"), scatter_dimension=0, tiled=True)
    gain_rows = gain_rows.reshape(4, d_half)
    return (
        block_out,
        tokens_grad,
        attn_grads[0],
        attn_grads[1],
        attn_grads[2],
        attn_grads[3].T,
        gate_weight_grad,
        up_weight_grad,
        down_weight_grad,
        gain_rows[0],
        gain_rows[1],
        gain_rows[2],
        gain_rows[3],
    )


def solution(mesh):
    in_specs = (
        P(("fsdp", "ctx"), None),
        P(("fsdp", "ctx"), None),
        P("fsdp", None),
        P("fsdp", None),
        P("fsdp", "tp"),
        P("fsdp", "tp"),
        P("fsdp", "tp"),
        P("tp", "fsdp"),
        P("fsdp", "tp"),
        P("fsdp", "tp"),
        P("tp", "fsdp"),
        P("fsdp"),
        P("fsdp"),
        P("fsdp"),
        P("fsdp"),
    )
    out_specs = (
        P(("fsdp", "ctx"), None),
        P(("fsdp", "ctx"), None),
        P(("fsdp", "ctx"), "tp"),
        P(("fsdp", "ctx"), "tp"),
        P(("fsdp", "ctx"), "tp"),
        P("tp", ("fsdp", "ctx")),
        P(("fsdp", "ctx"), "tp"),
        P(("fsdp", "ctx"), "tp"),
        P("tp", ("fsdp", "ctx")),
        P(("fsdp", "ctx")),
        P(("fsdp", "ctx")),
        P(("fsdp", "ctx")),
        P(("fsdp", "ctx")),
    )
    step = functools.partial(local, mesh.shape["fsdp"])
    return jax.shard_map(step, mesh=mesh, in_specs=in_specs, out_specs=out_specs, check_vma=False)
```

profile of v0, /device:TPU:0, one launch (start us, length us, event | category | flops | bytes accessed | tf_op | source)
XLA Modules:
  0.0 1150.1 jit_solution(1037541501683271396)
XLA Ops:
  15.2 31.4 %all-gather = f32[8,1,1152]{2,1,0:T(1,128)S(1)} all-gather(f32[1,1,1152]{2,1,0:T(1,128)S(1)} %bitcast_convert_fusion.2), channel_id=1, replica_groups=mesh['fsdp'=8,'ctx'=2,'tp'=2] {'fsdp'}, dimensions={0}, use_global_device_ids=true | all-gather | bytes 41472 | tf_op jit(solution)/shard_map/all_gather | solution.py:189
  53.8 40.0 %all-gather.4.cloned.1.call-done = bf16[2304,1024]{1,0:T(8,128)(2,1)} async-done(((bf16[288,1024]{1,0:T(8,128)(2,1)}), bf16[2304,1024]{1,0:T(8,128)(2,1)}) %all-gather.4.cloned.1.call-update) | async-done | bytes 4718608 | tf_op jit(solution)/shard_map/all_gather | solution.py:186
  108.9 37.8 %all-gather.6.cloned.1.call-done = bf16[2304,512]{1,0:T(8,128)(2,1)} async-done(((bf16[288,512]{1,0:T(8,128)(2,1)}), bf16[2304,512]{1,0:T(8,128)(2,1)}) %all-gather.6.cloned.1.call-update) | async-done | bytes 2359312 | tf_op jit(solution)/shard_map/all_gather | solution.py:188
  211.9 22.0 %collective-permute-done.5 = bf16[112,2304]{1,0:T(8,128)(2,1)S(1)} collective-permute-done((bf16[112,2304]{1,0:T(8,128)(2,1)S(1)}, bf16[112,2304]{1,0:T(8,128)(2,1)S(1)}, u32[]{:S(2)}, u32[]{:S(2)}) %collective-permute-start.5) | collective-permute-done | bytes 516128 | tf_op jit(solution)/shard_map/ppermute | solution.py:74
  271.4 21.1 %collective-permute-done.10 = bf16[112,2304]{1,0:T(8,128)(2,1)S(1)} collective-permute-done((bf16[112,2304]{1,0:T(8,128)(2,1)S(1)}, bf16[112,2304]{1,0:T(8,128)(2,1)S(1)}, u32[]{:S(2)}, u32[]{:S(2)}) %collective-permute-start.10) | collective-permute-done | bytes 516128 | tf_op jit(solution)/shard_map/ppermute | solution.py:74
  323.5 38.0 %collective-permute-done.19 = bf16[3,144,576]{2,1,0:T(8,128)(2,1)S(1)} collective-permute-done((bf16[3,144,576]{2,1,0:T(8,128)(2,1)}, bf16[3,144,576]{2,1,0:T(8,128)(2,1)S(1)}, u32[]{:S(2)}, u32[]{:S(2)}) %collective-permute-start.19) | collective-permute-done | bytes 497696 | tf_op jit(solution)/shard_map/ppermute | solution.py:74
  366.8 18.4 %collective-permute-done.21 = bf16[3,144,576]{2,1,0:T(8,128)(2,1)S(1)} collective-permute-done((bf16[3,144,576]{2,1,0:T(8,128)(2,1)}, bf16[3,144,576]{2,1,0:T(8,128)(2,1)S(1)}, u32[]{:S(2)}, u32[]{:S(2)}) %collective-permute-start.21) | collective-permute-done | bytes 497696 | tf_op jit(solution)/shard_map/ppermute | solution.py:74
  438.4 11.5 %fusion.192 = f32[1792,576]{0,1:T(8,128)} fusion(bf16[1792,2304]{1,0:T(8,128)(2,1)S(1)} %constant_dynamic-update-slice_fusion.8, bf16[2304,576]{1,0:T(8,128)(2,1)} %bitcast.35), kind=kOutput, calls=%fused_computation.456 | convolution fusion | flops 4756340736 | bytes 15040512 | tf_op jit(solution)/shard_map/dot_general | solution.py:66
  449.9 14.4 %multiply_convert_fusion.1 = (bf16[1792,576]{0,1:T(8,128)(2,1)}, f32[1792,576]{0,1:T(8,128)}) fusion(f32[1792,576]{0,1:T(8,128)} %fusion.192, bf16[1792,2304]{1,0:T(8,128)(2,1)} %copy-done.57, bf16[2304,576]{1,0:T(8,128)(2,1)} %bitcast.52), kind=kOutput, calls=%fused_computation.20 | convolution fusion | flops 4766662656 | bytes 21233664 | tf_op jit(solution)/shard_map/dot_general | solution.py:66
  504.5 11.1 collective-permute-done.32
  548.1 15.2 %collective-permute-done.30 = bf16[112,2304]{1,0:T(8,128)(2,1)S(1)} collective-permute-done((bf16[112,2304]{1,0:T(8,128)(2,1)}, bf16[112,2304]{1,0:T(8,128)(2,1)S(1)}, u32[]{:S(2)}, u32[]{:S(2)}) %collective-permute-start.30) | collective-permute-done | bytes 516128 | tf_op jit(solution)/shard_map/ppermute | solution.py:74
  573.5 18.7 %collective-permute-done.36 = bf16[112,2304]{1,0:T(8,128)(2,1)S(1)} collective-permute-done((bf16[112,2304]{1,0:T(8,128)(2,1)S(1)}, bf16[112,2304]{1,0:T(8,128)(2,1)S(1)}, u32[]{:S(2)}, u32[]{:S(2)}) %collective-permute-start.36) | collective-permute-done | bytes 516128 | tf_op jit(solution)/shard_map/ppermute | solution.py:74
  594.4 11.5 collective-permute-done.38
  641.3 12.4 %fusion.3 = (bf16[1792,576]{0,1:T(8,128)(2,1)S(1)}, bf16[1792,576]{0,1:T(8,128)(2,1)S(1)}) fusion(f32[1792,576]{0,1:T(8,128)S(1)} %copy-done.81, f32[1792,576]{0,1:T(8,128)} %get-tuple-element.226, bf16[1792,2304]{1,0:T(8,128)(2,1)} %copy-done.55, bf16[2304,576]{1,0:T(8,128)(2,1)S(1)} %bitcast.455), kind=kOutput, calls=%fused_computation.16 | convolution fusion | flops 4785242112 | bytes 23298048 | tf_op jit(solution)/shard_map/dot_general | solution.py:66
  653.7 13.6 %fusion.194 = f32[1792,2304]{1,0:T(8,128)} fusion(bf16[1792,576]{0,1:T(8,128)(2,1)S(1)} %get-tuple-element.63, bf16[2304,576]{1,0:T(8,128)(2,1)} %bitcast.52), kind=kOutput, calls=%fused_computation.458 | convolution fusion | flops 4756340736 | bytes 21233664 | tf_op jit(solution)/shard_map/dot_general | solution.py:66
  667.3 15.2 %convolution_add_fusion = f32[1792,2304]{1,0:T(8,128)} fusion(f32[1792,2304]{1,0:T(8,128)} %fusion.194, bf16[1792,576]{0,1:T(8,128)(2,1)S(1)} %get-tuple-element.62, bf16[2304,576]{1,0:T(8,128)(2,1)} %bitcast.35), kind=kOutput, calls=%fused_computation | convolution fusion | flops 4760469504 | bytes 37748736 | tf_op jit(solution)/shard_map/dot_general | solution.py:66
  709.0 11.1 collective-permute-done.49
  731.2 11.1 collective-permute-done.48
  752.5 14.1 %collective-permute-done.47 = bf16[112,2304]{1,0:T(8,128)(2,1)S(1)} collective-permute-done((bf16[112,2304]{1,0:T(8,128)(2,1)S(1)}, bf16[112,2304]{1,0:T(8,128)(2,1)S(1)}, u32[]{:S(2)}, u32[]{:S(2)}) %collective-permute-start.47) | collective-permute-done | bytes 516128 | tf_op jit(solution)/shard_map/ppermute | solution.py:74
  865.8 28.8 %collective-permute-done.60 = bf16[8,144,576]{2,1,0:T(8,128)(2,1)} collective-permute-done((bf16[8,144,576]{2,1,0:T(8,128)(2,1)}, bf16[8,144,576]{2,1,0:T(8,128)(2,1)}, u32[]{:S(2)}, u32[]{:S(2)}) %collective-permute-start.60) | collective-permute-done | bytes 1327136 | tf_op jit(solution)/shard_map/ppermute | solution.py:70
  897.2 28.2 %collective-permute-done.61 = bf16[8,144,576]{2,1,0:T(8,128)(2,1)} collective-permute-done((bf16[8,144,576]{2,1,0:T(8,128)(2,1)}, bf16[8,144,576]{2,1,0:T(8,128)(2,1)}, u32[]{:S(2)}, u32[]{:S(2)}) %collective-permute-start.61) | collective-permute-done | bytes 1327136 | tf_op jit(solution)/shard_map/ppermute | solution.py:70
  959.9 16.9 %collective-permute-done.63 = bf16[3,144,576]{2,1,0:T(8,128)(2,1)S(1)} collective-permute-done((bf16[3,144,576]{2,1,0:T(8,128)(2,1)S(1)}, bf16[3,144,576]{2,1,0:T(8,128)(2,1)S(1)}, u32[]{:S(2)}, u32[]{:S(2)}) %collective-permute-start.63) | collective-permute-done | bytes 497696 | tf_op jit(solution)/shard_map/ppermute | solution.py:74
  978.4 11.1 collective-permute-done.64
  1038.3 90.6 %all-reduce = f32[16,576]{1,0:T(8,128)S(1)} all-reduce(f32[16,576]{1,0:T(8,128)S(1)} %add.561), channel_id=3, replica_groups=mesh['fsdp'=8,'ctx'=2,'tp'=2] {'fsdp','ctx'}, use_global_device_ids=true, to_apply=%region_17.18.clone | all-reduce | flops 9216 | bytes 73728
  (511 shorter events, 589.6 us)
Async XLA Ops:
  7.3 86.5 %all-gather.4.cloned.1.call-start = ((), (), s32[]{:S(2)}) async-start(), calls=%async_computation.1 | async-start | bytes 5308416 | tf_op jit(solution)/shard_map/all_gather | solution.py:186
  10.2 136.4 %all-gather.6.cloned.1.call-start = ((), (), s32[]{:S(2)}) async-start(), calls=%async_computation.2 | async-start | bytes 2654208 | tf_op jit(solution)/shard_map/all_gather | solution.py:188
  10.3 37.3 %collective-permute-start = (bf16[112,2304]{1,0:T(8,128)(2,1)S(1)}, bf16[112,2304]{1,0:T(8,128)(2,1)S(1)}, u32[]{:S(2)}, u32[]{:S(2)}) collective-permute-start(bf16[112,2304]{1,0:T(8,128)(2,1)S(1)} %constant_dynamic-slice_fusion.11), channel_id=1, source_target_pairs={{0,2},{2,0},{1,3},{3,1},{4,6},{6,4},{5,7},{7,5},{8,10},{10,8},{9,1... | collective-permute-start | bytes 1548296 | tf_op jit(solution)/shard_map/ppermute | solution.py:70
  14.1 1116.0 %reduce-scatter.4.cloned.1.call-start = ((), (), s32[]{:S(2)}) async-start(), calls=%async_computation.3 | async-start | bytes 7962624 | tf_op jit(solution)/shard_map/reduce_scatter | solution.py:305
  198.0 114.1 %collective-permute-start.12 = (bf16[3,144,576]{2,1,0:T(8,128)(2,1)S(1)}, bf16[3,144,576]{2,1,0:T(8,128)(2,1)}, u32[]{:S(2)}, u32[]{:S(2)}) collective-permute-start(bf16[3,144,576]{2,1,0:T(8,128)(2,1)S(1)} %bitcast.457), channel_id=1, source_target_pairs={{0,2},{2,0},{1,3},{3,1},{4,6},{6,4},{5,7},{7,5},{8,10},{10,8},{9,1... | collective-permute-start | bytes 1493000 | tf_op jit(solution)/shard_map/ppermute | solution.py:70
  199.6 100.0 %collective-permute-start.13 = (bf16[3,144,576]{2,1,0:T(8,128)(2,1)S(1)}, bf16[3,144,576]{2,1,0:T(8,128)(2,1)}, u32[]{:S(2)}, u32[]{:S(2)}) collective-permute-start(bf16[3,144,576]{2,1,0:T(8,128)(2,1)S(1)} %bitcast.466), channel_id=1, source_target_pairs={{0,4},{4,0},{8,12},{12,8},{16,20},{20,16},{24,28},{28,24},{1,5},{5... | collective-permute-start | bytes 1493000 | tf_op jit(solution)/shard_map/ppermute | solution.py:74
  201.1 111.1 %collective-permute-start.15 = (bf16[3,144,576]{2,1,0:T(8,128)(2,1)}, bf16[3,144,576]{2,1,0:T(8,128)(2,1)}, u32[]{:S(2)}, u32[]{:S(2)}) collective-permute-start(bf16[3,144,576]{2,1,0:T(8,128)(2,1)} %bitcast.438), channel_id=1, source_target_pairs={{0,8},{4,12},{8,0},{12,4},{16,24},{20,28},{24,16},{28,20},{1,9},{5... | collective-permute-start | bytes 1493000 | tf_op jit(solution)/shard_map/ppermute | solution.py:74
  270.5 51.1 %collective-permute-start.17 = (bf16[3,144,576]{2,1,0:T(8,128)(2,1)S(1)}, bf16[3,144,576]{2,1,0:T(8,128)(2,1)}, u32[]{:S(2)}, u32[]{:S(2)}) collective-permute-start(bf16[3,144,576]{2,1,0:T(8,128)(2,1)S(1)} %bitcast.465), channel_id=1, source_target_pairs={{0,12},{4,8},{8,4},{12,0},{16,28},{20,24},{24,20},{28,16},{1,13},{... | collective-permute-start | bytes 1493000 | tf_op jit(solution)/shard_map/ppermute | solution.py:74
  293.3 142.6 %collective-permute-start.11 = (bf16[896,2304]{1,0:T(8,128)(2,1)}, bf16[896,2304]{1,0:T(8,128)(2,1)}, u32[]{:S(2)}, u32[]{:S(2)}) collective-permute-start(bf16[896,2304]{1,0:T(8,128)(2,1)} %get-tuple-element.191), channel_id=1, source_target_pairs={{0,1},{1,0},{2,3},{3,2},{4,5},{5,4},{6,7},{7,6},{8,9},{9,8},{10,11... | collective-permute-start | bytes 12386312 | tf_op jit(solution)/shard_map/ppermute | solution.py:70
  312.1 49.4 %collective-permute-start.19 = (bf16[3,144,576]{2,1,0:T(8,128)(2,1)}, bf16[3,144,576]{2,1,0:T(8,128)(2,1)S(1)}, u32[]{:S(2)}, u32[]{:S(2)}) collective-permute-start(bf16[3,144,576]{2,1,0:T(8,128)(2,1)} %bitcast.470), channel_id=1, source_target_pairs={{0,16},{4,20},{8,24},{12,28},{16,0},{20,4},{24,8},{28,12},{1,17},{... | collective-permute-start | bytes 1493000 | tf_op jit(solution)/shard_map/ppermute | solution.py:74
  312.2 51.3 %collective-permute-start.16 = (bf16[3,144,576]{2,1,0:T(8,128)(2,1)}, bf16[3,144,576]{2,1,0:T(8,128)(2,1)S(1)}, u32[]{:S(2)}, u32[]{:S(2)}) collective-permute-start(bf16[3,144,576]{2,1,0:T(8,128)(2,1)} %collective-permute-done.15), channel_id=1, source_target_pairs={{0,2},{2,0},{1,3},{3,1},{4,6},{6,4},{5,7},{7,5},{8,10},{10,8},{9,1... | collective-permute-start | bytes 1493000 | tf_op jit(solution)/shard_map/ppermute | solution.py:70
  316.9 68.3 %collective-permute-start.21 = (bf16[3,144,576]{2,1,0:T(8,128)(2,1)}, bf16[3,144,576]{2,1,0:T(8,128)(2,1)S(1)}, u32[]{:S(2)}, u32[]{:S(2)}) collective-permute-start(bf16[3,144,576]{2,1,0:T(8,128)(2,1)} %bitcast.469), channel_id=1, source_target_pairs={{0,20},{4,16},{8,28},{12,24},{16,4},{20,0},{24,12},{28,8},{1,21},{... | collective-permute-start | bytes 1493000 | tf_op jit(solution)/shard_map/ppermute | solution.py:74
  321.6 66.0 %collective-permute-start.23 = (bf16[3,144,576]{2,1,0:T(8,128)(2,1)S(1)}, bf16[3,144,576]{2,1,0:T(8,128)(2,1)S(1)}, u32[]{:S(2)}, u32[]{:S(2)}) collective-permute-start(bf16[3,144,576]{2,1,0:T(8,128)(2,1)S(1)} %bitcast.468), channel_id=1, source_target_pairs={{0,24},{4,28},{8,16},{12,20},{16,8},{20,12},{24,0},{28,4},{1,25},{... | collective-permute-start | bytes 1493000 | tf_op jit(solution)/shard_map/ppermute | solution.py:74
  389.7 45.4 %collective-permute-start.26 = (bf16[3,144,576]{2,1,0:T(8,128)(2,1)S(1)}, bf16[3,144,576]{2,1,0:T(8,128)(2,1)S(1)}, u32[]{:S(2)}, u32[]{:S(2)}) collective-permute-start(bf16[3,144,576]{2,1,0:T(8,128)(2,1)S(1)} %collective-permute-done.25), channel_id=1, source_target_pairs={{0,2},{2,0},{1,3},{3,1},{4,6},{6,4},{5,7},{7,5},{8,10},{10,8},{9,1... | collective-permute-start | bytes 1493000 | tf_op jit(solution)/shard_map/ppermute | solution.py:70
  841.1 53.4 %collective-permute-start.60 = (bf16[8,144,576]{2,1,0:T(8,128)(2,1)}, bf16[8,144,576]{2,1,0:T(8,128)(2,1)}, u32[]{:S(2)}, u32[]{:S(2)}) collective-permute-start(bf16[8,144,576]{2,1,0:T(8,128)(2,1)} %fusion.25), channel_id=1, source_target_pairs={{0,2},{2,0},{1,3},{3,1},{4,6},{6,4},{5,7},{7,5},{8,10},{10,8},{9,1... | collective-permute-start | bytes 3981320 | tf_op jit(solution)/shard_map/ppermute | solution.py:70
  852.2 73.1 %collective-permute-start.61 = (bf16[8,144,576]{2,1,0:T(8,128)(2,1)}, bf16[8,144,576]{2,1,0:T(8,128)(2,1)}, u32[]{:S(2)}, u32[]{:S(2)}) collective-permute-start(bf16[8,144,576]{2,1,0:T(8,128)(2,1)} %fusion.26), channel_id=1, source_target_pairs={{0,2},{2,0},{1,3},{3,1},{4,6},{6,4},{5,7},{7,5},{8,10},{10,8},{9,1... | collective-permute-start | bytes 3981320 | tf_op jit(solution)/shard_map/ppermute | solution.py:70
  858.0 72.8 %collective-permute-start.54 = (f32[224,2304]{1,0:T(8,128)}, f32[224,2304]{1,0:T(8,128)}, u32[]{:S(2)}, u32[]{:S(2)}) collective-permute-start(f32[224,2304]{1,0:T(8,128)} %pad_maximum_fusion.4), channel_id=1, source_target_pairs={{0,1},{1,0},{2,3},{3,2},{4,5},{5,4},{6,7},{7,6},{8,9},{9,8},{10,11... | collective-permute-start | bytes 6193160 | tf_op jit(solution)/shard_map/ppermute | solution.py:70
  858.7 74.2 %collective-permute-start.35 = (bf16[112,2304]{1,0:T(8,128)(2,1)}, bf16[112,2304]{1,0:T(8,128)(2,1)S(1)}, u32[]{:S(2)}, u32[]{:S(2)}) collective-permute-start(bf16[112,2304]{1,0:T(8,128)(2,1)} %get-tuple-element.92), channel_id=1, source_target_pairs={{0,1},{1,0},{2,3},{3,2},{4,5},{5,4},{6,7},{7,6},{8,9},{9,8},{10,11... | collective-permute-start | bytes 1548296 | tf_op jit(solution)/shard_map/ppermute | solution.py:70
  935.5 41.3 %collective-permute-start.63 = (bf16[3,144,576]{2,1,0:T(8,128)(2,1)S(1)}, bf16[3,144,576]{2,1,0:T(8,128)(2,1)S(1)}, u32[]{:S(2)}, u32[]{:S(2)}) collective-permute-start(bf16[3,144,576]{2,1,0:T(8,128)(2,1)S(1)} %get-tuple-element.71), channel_id=1, source_target_pairs={{0,8},{4,12},{8,0},{12,4},{16,24},{20,28},{24,16},{28,20},{1,9},{5... | collective-permute-start | bytes 1493000 | tf_op jit(solution)/shard_map/ppermute | solution.py:74
  937.4 52.0 %collective-permute-start.64 = (bf16[3,144,576]{2,1,0:T(8,128)(2,1)S(1)}, bf16[3,144,576]{2,1,0:T(8,128)(2,1)S(1)}, u32[]{:S(2)}, u32[]{:S(2)}) collective-permute-start(bf16[3,144,576]{2,1,0:T(8,128)(2,1)S(1)} %get-tuple-element.70), channel_id=1, source_target_pairs={{0,12},{4,8},{8,4},{12,0},{16,28},{20,24},{24,20},{28,16},{1,13},{... | collective-permute-start | bytes 1493000 | tf_op jit(solution)/shard_map/ppermute | solution.py:74
  938.1 53.5 %collective-permute-start.65 = (bf16[3,144,576]{2,1,0:T(8,128)(2,1)S(1)}, bf16[3,144,576]{2,1,0:T(8,128)(2,1)S(1)}, u32[]{:S(2)}, u32[]{:S(2)}) collective-permute-start(bf16[3,144,576]{2,1,0:T(8,128)(2,1)S(1)} %get-tuple-element.69), channel_id=1, source_target_pairs={{0,16},{4,20},{8,24},{12,28},{16,0},{20,4},{24,8},{28,12},{1,17},{... | collective-permute-start | bytes 1493000 | tf_op jit(solution)/shard_map/ppermute | solution.py:74
  943.3 49.5 %collective-permute-start.66 = (bf16[3,144,576]{2,1,0:T(8,128)(2,1)S(1)}, bf16[3,144,576]{2,1,0:T(8,128)(2,1)S(1)}, u32[]{:S(2)}, u32[]{:S(2)}) collective-permute-start(bf16[3,144,576]{2,1,0:T(8,128)(2,1)S(1)} %get-tuple-element.68), channel_id=1, source_target_pairs={{0,20},{4,16},{8,28},{12,24},{16,4},{20,0},{24,12},{28,8},{1,21},{... | collective-permute-start | bytes 1493000 | tf_op jit(solution)/shard_map/ppermute | solution.py:74
  956.1 47.1 %collective-permute-start.67 = (bf16[3,144,576]{2,1,0:T(8,128)(2,1)S(1)}, bf16[3,144,576]{2,1,0:T(8,128)(2,1)S(1)}, u32[]{:S(2)}, u32[]{:S(2)}) collective-permute-start(bf16[3,144,576]{2,1,0:T(8,128)(2,1)S(1)} %get-tuple-element.67), channel_id=1, source_target_pairs={{0,24},{4,28},{8,16},{12,20},{16,8},{20,12},{24,0},{28,4},{1,25},{... | collective-permute-start | bytes 1493000 | tf_op jit(solution)/shard_map/ppermute | solution.py:74
  992.8 138.5 %collective-permute-start.57 = (bf16[224,2304]{1,0:T(8,128)(2,1)}, bf16[224,2304]{1,0:T(8,128)(2,1)}, u32[]{:S(2)}, u32[]{:S(2)}) collective-permute-start(bf16[224,2304]{1,0:T(8,128)(2,1)} %pad_maximum_fusion.7), channel_id=1, source_target_pairs={{0,1},{1,0},{2,3},{3,2},{4,5},{5,4},{6,7},{7,6},{8,9},{9,8},{10,11... | collective-permute-start | bytes 3096584 | tf_op jit(solution)/shard_map/ppermute | solution.py:70
  (139 other events, 2471.9 us)
Sparse Core Ops, SparseCore 0:
  10.9 82.8 all-gather.3
  96.5 50.0 all-gather.5
  815.2 151.4 reduce-scatter.3
where the time goes:
time: 1160 us; the launch traced here: 1150 us
  waiting for transfers between devices  571 us (49%)
  local copies, waits for them, and re-layouts  158 us (14%)
  matrix products  132 us (11%)
  blocking collectives  122 us (11%)
  other arithmetic  80.2 us (7%)
  starting transfers between devices  71.3 us (6%)
  between operations  16.4 us (1%)
    ppermute x42, waiting for transfers between devices, hop(): return lax.ppermute(piece, 'fsdp', [(d, d ^ step) for d in range(n)])  338 us
    ppermute x28, waiting for transfers between devices, swap(): return lax.ppermute(piece, axis, [(0, 1), (1, 0)])  155 us
    dot_general x17, matrix products, dot(): lax.dot_general(lhs, rhs, (dims, ((), ())), preferred_element_type=f32)  125 us
    unnamed x1, blocking collectives  90.6 us
    unnamed x207, local copies, waits for them, and re-layouts  58.9 us
    ppermute x42, starting transfers between devices, hop(): return lax.ppermute(piece, 'fsdp', [(d, d ^ step) for d in range(n)])  51.9 us
    all_gather x1, waiting for transfers between devices, local(): qkv_weight = lax.all_gather(qkv_own, 'fsdp', axis=0, tiled=True)  40 us
    all_gather x1, waiting for transfers between devices, local(): out_weight = lax.all_gather(out_own, 'fsdp', axis=0, tiled=True)  37.8 us
  transfers between devices with their start and end apart: 73, of which 48 were waited for; matrix products, arithmetic and copies ran while one was open for 16% of the time, Pallas kernels for 0%

commit v1 on v0

--- a/solution.py
+++ b/solution.py
@@ -183,7 +183,12 @@
         ],
         axis=1,
     )
-    qkv_weight = lax.all_gather(qkv_own, "fsdp", axis=0, tiled=True)
+    ring = [qkv_own]
+    for hop_ in range(7):
+        ring.append(lax.ppermute(ring[-1], "fsdp", [(dev, (dev + 1) % 8) for dev in range(8)]))
+    qkv_weight = jnp.roll(
+        jnp.concatenate(ring[::-1], axis=0), (lax.axis_index("fsdp") + 1) * ring[0].shape[0], axis=0
+    )
     out_own = lax.dynamic_slice_in_dim(output_weight, ctx * q_cols, q_cols, 0).T
     out_weight = lax.all_gather(out_own, "fsdp", axis=0, tiled=True)
     gains = lax.all_gather(

time: 1160 us -> 1200 us (1.034)
  waiting for transfers between devices: 571 us -> 596 us
  blocking collectives: 122 us -> 137 us
    ppermute x0 -> x7, waiting for transfers between devices: none -> 100 us  [local(): lax.ppermute(ring[-1], 'fsdp', [(dev, (dev + 1) % 8) for dev in range(8)])]
    all_gather x1 -> x0, waiting for transfers between devices: 40 us -> none  [local(): qkv_weight = lax.all_gather(qkv_own, 'fsdp', axis=0, tiled=True)]
    all_gather x1, waiting for transfers between devices: 37.8 us -> 0.02 us  [local(): out_weight = lax.all_gather(out_own, 'fsdp', axis=0, tiled=True)]
    all_gather x1, blocking collectives: 31.4 us -> 53.3 us  [local(): lax.all_gather(jnp.concatenate([gain_attn_in, gain_attn_out, gain_ffn_in,...]
    unnamed x207 -> x225, local copies, waits for them, and re-layouts: 58.9 us -> 65.4 us
  transfers between devices with their start and end apart: 73 -> 79, of which waited for: 48 -> 51; matrix products, arithmetic and copies ran while one was open for 16% -> 15% of each run, Pallas kernels for 0% -> 0%
where the time goes in v1:
time: 1200 us
  waiting for transfers between devices  596 us (50%)
  local copies, waits for them, and re-layouts  166 us (14%)
  blocking collectives  137 us (11%)
  matrix products  128 us (11%)
  other arithmetic  79 us (7%)
  starting transfers between devices  73.1 us (6%)
  between operations  17 us (1%)
    ppermute x42, waiting for transfers between devices, hop(): return lax.ppermute(piece, 'fsdp', [(d, d ^ step) for d in range(n)])  339 us
    ppermute x28, waiting for transfers between devices, swap(): return lax.ppermute(piece, axis, [(0, 1), (1, 0)])  156 us
    dot_general x17, matrix products, dot(): lax.dot_general(lhs, rhs, (dims, ((), ())), preferred_element_type=f32)  121 us
    ppermute x7, waiting for transfers between devices, local(): lax.ppermute(ring[-1], 'fsdp', [(dev, (dev + 1) % 8) for dev in range(8)])  100 us
    unnamed x1, blocking collectives  83.3 us
    unnamed x225, local copies, waits for them, and re-layouts  65.4 us
    all_gather x1, blocking collectives, local(): lax.all_gather(jnp.concatenate([gain_attn_in, gain_attn_out, gain_ffn_in,...  53.3 us
    ppermute x42, starting transfers between devices, hop(): return lax.ppermute(piece, 'fsdp', [(d, d ^ step) for d in range(n)])  52.5 us
  transfers between devices with their start and end apart: 79, of which 51 were waited for; matrix products, arithmetic and copies ran while one was open for 15% of the time, Pallas kernels for 0%

profile of v1, /device:TPU:0, one launch (start us, length us, event | category | flops | bytes accessed | tf_op | source)
XLA Modules:
  0.0 1195.2 jit_solution(10672512387005342821)
XLA Ops:
  12.4 16.4 %collective-permute-done.2 = bf16[288,1024]{1,0:T(8,128)(2,1)S(1)} collective-permute-done((bf16[288,1024]{1,0:T(8,128)(2,1)S(1)}, bf16[288,1024]{1,0:T(8,128)(2,1)S(1)}, u32[]{:S(2)}, u32[]{:S(2)}) %collective-permute-start.2) | collective-permute-done | bytes 589856 | tf_op jit(solution)/shard_map/ppermute | solution.py:188
  28.8 17.2 %collective-permute-done.3 = bf16[288,1024]{1,0:T(8,128)(2,1)S(1)} collective-permute-done((bf16[288,1024]{1,0:T(8,128)(2,1)S(1)}, bf16[288,1024]{1,0:T(8,128)(2,1)S(1)}, u32[]{:S(2)}, u32[]{:S(2)}) %collective-permute-start.3) | collective-permute-done | bytes 589856 | tf_op jit(solution)/shard_map/ppermute | solution.py:188
  50.0 12.4 %collective-permute-done.4 = bf16[288,1024]{1,0:T(8,128)(2,1)S(1)} collective-permute-done((bf16[288,1024]{1,0:T(8,128)(2,1)S(1)}, bf16[288,1024]{1,0:T(8,128)(2,1)S(1)}, u32[]{:S(2)}, u32[]{:S(2)}) %collective-permute-start.4) | collective-permute-done | bytes 589856 | tf_op jit(solution)/shard_map/ppermute | solution.py:188
  62.6 23.8 %collective-permute-done.5 = bf16[288,1024]{1,0:T(8,128)(2,1)S(1)} collective-permute-done((bf16[288,1024]{1,0:T(8,128)(2,1)S(1)}, bf16[288,1024]{1,0:T(8,128)(2,1)S(1)}, u32[]{:S(2)}, u32[]{:S(2)}) %collective-permute-start.5) | collective-permute-done | bytes 589856 | tf_op jit(solution)/shard_map/ppermute | solution.py:188
  87.2 53.3 %all-gather = f32[8,1,1152]{2,1,0:T(1,128)S(1)} all-gather(f32[1,1,1152]{2,1,0:T(1,128)S(1)} %bitcast_convert_fusion.2), channel_id=1, replica_groups=mesh['fsdp'=8,'ctx'=2,'tp'=2] {'fsdp'}, dimensions={0}, use_global_device_ids=true | all-gather | bytes 41472 | tf_op jit(solution)/shard_map/all_gather | solution.py:194
  144.0 15.8 %collective-permute-done.7 = bf16[288,1024]{1,0:T(8,128)(2,1)} collective-permute-done((bf16[288,1024]{1,0:T(8,128)(2,1)}, bf16[288,1024]{1,0:T(8,128)(2,1)}, u32[]{:S(2)}, u32[]{:S(2)}) %collective-permute-start.7) | collective-permute-done | bytes 589856 | tf_op jit(solution)/shard_map/ppermute | solution.py:188
  162.7 14.8 %collective-permute-done.8 = bf16[288,1024]{1,0:T(8,128)(2,1)S(1)} collective-permute-done((bf16[288,1024]{1,0:T(8,128)(2,1)}, bf16[288,1024]{1,0:T(8,128)(2,1)S(1)}, u32[]{:S(2)}, u32[]{:S(2)}) %collective-permute-start.8) | collective-permute-done | bytes 589856 | tf_op jit(solution)/shard_map/ppermute | solution.py:188
  255.7 22.0 %collective-permute-done.12 = bf16[112,2304]{1,0:T(8,128)(2,1)S(1)} collective-permute-done((bf16[112,2304]{1,0:T(8,128)(2,1)S(1)}, bf16[112,2304]{1,0:T(8,128)(2,1)S(1)}, u32[]{:S(2)}, u32[]{:S(2)}) %collective-permute-start.12) | collective-permute-done | bytes 516128 | tf_op jit(solution)/shard_map/ppermute | solution.py:74
  317.1 20.4 %collective-permute-done.17 = bf16[112,2304]{1,0:T(8,128)(2,1)S(1)} collective-permute-done((bf16[112,2304]{1,0:T(8,128)(2,1)S(1)}, bf16[112,2304]{1,0:T(8,128)(2,1)S(1)}, u32[]{:S(2)}, u32[]{:S(2)}) %collective-permute-start.17) | collective-permute-done | bytes 516128 | tf_op jit(solution)/shard_map/ppermute | solution.py:74
  369.0 37.5 %collective-permute-done.26 = bf16[3,144,576]{2,1,0:T(8,128)(2,1)S(1)} collective-permute-done((bf16[3,144,576]{2,1,0:T(8,128)(2,1)}, bf16[3,144,576]{2,1,0:T(8,128)(2,1)S(1)}, u32[]{:S(2)}, u32[]{:S(2)}) %collective-permute-start.26) | collective-permute-done | bytes 497696 | tf_op jit(solution)/shard_map/ppermute | solution.py:74
  413.0 18.1 %collective-permute-done.28 = bf16[3,144,576]{2,1,0:T(8,128)(2,1)S(1)} collective-permute-done((bf16[3,144,576]{2,1,0:T(8,128)(2,1)}, bf16[3,144,576]{2,1,0:T(8,128)(2,1)S(1)}, u32[]{:S(2)}, u32[]{:S(2)}) %collective-permute-start.28) | collective-permute-done | bytes 497696 | tf_op jit(solution)/shard_map/ppermute | solution.py:74
  495.8 14.4 %multiply_convert_fusion.1 = (bf16[1792,576]{0,1:T(8,128)(2,1)}, f32[1792,576]{0,1:T(8,128)}) fusion(f32[1792,576]{0,1:T(8,128)} %fusion.196, bf16[1792,2304]{1,0:T(8,128)(2,1)} %copy-done.58, bf16[2304,576]{1,0:T(8,128)(2,1)} %bitcast.52), kind=kOutput, calls=%fused_computation.24 | convolution fusion | flops 4766662656 | bytes 21233664 | tf_op jit(solution)/shard_map/dot_general | solution.py:66
  549.3 12.0 %collective-permute-done.39 = bf16[112,2304]{1,0:T(8,128)(2,1)S(1)} collective-permute-done((bf16[112,2304]{1,0:T(8,128)(2,1)S(1)}, bf16[112,2304]{1,0:T(8,128)(2,1)S(1)}, u32[]{:S(2)}, u32[]{:S(2)}) %collective-permute-start.39) | collective-permute-done | bytes 516128 | tf_op jit(solution)/shard_map/ppermute | solution.py:74
  593.8 15.4 %collective-permute-done.37 = bf16[112,2304]{1,0:T(8,128)(2,1)S(1)} collective-permute-done((bf16[112,2304]{1,0:T(8,128)(2,1)}, bf16[112,2304]{1,0:T(8,128)(2,1)S(1)}, u32[]{:S(2)}, u32[]{:S(2)}) %collective-permute-start.37) | collective-permute-done | bytes 516128 | tf_op jit(solution)/shard_map/ppermute | solution.py:74
  618.6 19.6 %collective-permute-done.43 = bf16[112,2304]{1,0:T(8,128)(2,1)S(1)} collective-permute-done((bf16[112,2304]{1,0:T(8,128)(2,1)S(1)}, bf16[112,2304]{1,0:T(8,128)(2,1)S(1)}, u32[]{:S(2)}, u32[]{:S(2)}) %collective-permute-start.43) | collective-permute-done | bytes 516128 | tf_op jit(solution)/shard_map/ppermute | solution.py:74
  687.2 12.4 %fusion.7 = (bf16[1792,576]{0,1:T(8,128)(2,1)S(1)}, bf16[1792,576]{0,1:T(8,128)(2,1)S(1)}) fusion(f32[1792,576]{0,1:T(8,128)S(1)} %copy-done.82, f32[1792,576]{0,1:T(8,128)} %get-tuple-element.226, bf16[1792,2304]{1,0:T(8,128)(2,1)} %copy-done.56, bf16[2304,576]{1,0:T(8,128)(2,1)S(1)} %bitcast.453), kind=kOutput, calls=%fused_computation.20 | convolution fusion | flops 4785242112 | bytes 23298048 | tf_op jit(solution)/shard_map/dot_general | solution.py:66
  699.6 13.6 %fusion.198 = f32[1792,2304]{1,0:T(8,128)} fusion(bf16[1792,576]{0,1:T(8,128)(2,1)S(1)} %get-tuple-element.63, bf16[2304,576]{1,0:T(8,128)(2,1)} %bitcast.52), kind=kOutput, calls=%fused_computation.478 | convolution fusion | flops 4756340736 | bytes 21233664 | tf_op jit(solution)/shard_map/dot_general | solution.py:66
  713.2 15.1 %convolution_add_fusion = f32[1792,2304]{1,0:T(8,128)} fusion(f32[1792,2304]{1,0:T(8,128)} %fusion.198, bf16[1792,576]{0,1:T(8,128)(2,1)S(1)} %get-tuple-element.62, bf16[2304,576]{1,0:T(8,128)(2,1)} %bitcast.35), kind=kOutput, calls=%fused_computation | convolution fusion | flops 4760469504 | bytes 37748736 | tf_op jit(solution)/shard_map/dot_general | solution.py:66
  798.2 14.0 %collective-permute-done.54 = bf16[112,2304]{1,0:T(8,128)(2,1)S(1)} collective-permute-done((bf16[112,2304]{1,0:T(8,128)(2,1)S(1)}, bf16[112,2304]{1,0:T(8,128)(2,1)S(1)}, u32[]{:S(2)}, u32[]{:S(2)}) %collective-permute-start.54) | collective-permute-done | bytes 516128 | tf_op jit(solution)/shard_map/ppermute | solution.py:74
  911.4 28.8 %collective-permute-done.67 = bf16[8,144,576]{2,1,0:T(8,128)(2,1)} collective-permute-done((bf16[8,144,576]{2,1,0:T(8,128)(2,1)}, bf16[8,144,576]{2,1,0:T(8,128)(2,1)}, u32[]{:S(2)}, u32[]{:S(2)}) %collective-permute-start.67) | collective-permute-done | bytes 1327136 | tf_op jit(solution)/shard_map/ppermute | solution.py:70
  942.9 28.1 %collective-permute-done.68 = bf16[8,144,576]{2,1,0:T(8,128)(2,1)} collective-permute-done((bf16[8,144,576]{2,1,0:T(8,128)(2,1)}, bf16[8,144,576]{2,1,0:T(8,128)(2,1)}, u32[]{:S(2)}, u32[]{:S(2)}) %collective-permute-start.68) | collective-permute-done | bytes 1327136 | tf_op jit(solution)/shard_map/ppermute | solution.py:70
  1005.5 16.2 %collective-permute-done.70 = bf16[3,144,576]{2,1,0:T(8,128)(2,1)S(1)} collective-permute-done((bf16[3,144,576]{2,1,0:T(8,128)(2,1)S(1)}, bf16[3,144,576]{2,1,0:T(8,128)(2,1)S(1)}, u32[]{:S(2)}, u32[]{:S(2)}) %collective-permute-start.70) | collective-permute-done | bytes 497696 | tf_op jit(solution)/shard_map/ppermute | solution.py:74
  1037.4 22.8 %collective-permute-done.73 = bf16[3,144,576]{2,1,0:T(8,128)(2,1)S(1)} collective-permute-done((bf16[3,144,576]{2,1,0:T(8,128)(2,1)S(1)}, bf16[3,144,576]{2,1,0:T(8,128)(2,1)S(1)}, u32[]{:S(2)}, u32[]{:S(2)}) %collective-permute-start.73) | collective-permute-done | bytes 497696 | tf_op jit(solution)/shard_map/ppermute | solution.py:74
  1090.3 83.3 %all-reduce = f32[16,576]{1,0:T(8,128)S(1)} all-reduce(f32[16,576]{1,0:T(8,128)S(1)} %add.577), channel_id=3, replica_groups=mesh['fsdp'=8,'ctx'=2,'tp'=2] {'fsdp','ctx'}, use_global_device_ids=true, to_apply=%region_17.18.clone | all-reduce | flops 9216 | bytes 73728
  (542 shorter events, 630.8 us)
Async XLA Ops:
  7.3 188.4 %all-gather.3.cloned.1.call-start = ((), (), s32[]{:S(2)}) async-start(), calls=%async_computation.1 | async-start | bytes 2654208 | tf_op jit(solution)/shard_map/all_gather | solution.py:193
  47.8 93.1 %collective-permute-start = (bf16[112,2304]{1,0:T(8,128)(2,1)}, bf16[112,2304]{1,0:T(8,128)(2,1)}, u32[]{:S(2)}, u32[]{:S(2)}) collective-permute-start(bf16[112,2304]{1,0:T(8,128)(2,1)} %constant_dynamic-slice_fusion.11), channel_id=1, source_target_pairs={{0,2},{2,0},{1,3},{3,1},{4,6},{6,4},{5,7},{7,5},{8,10},{10,8},{9,1... | collective-permute-start | bytes 1548296 | tf_op jit(solution)/shard_map/ppermute | solution.py:70
  49.9 1125.0 %reduce-scatter.4.cloned.1.call-start = ((), (), s32[]{:S(2)}) async-start(), calls=%async_computation.2 | async-start | bytes 7962624 | tf_op jit(solution)/shard_map/reduce_scatter | solution.py:310
  86.4 54.6 %collective-permute-start.6 = (bf16[288,1024]{1,0:T(8,128)(2,1)S(1)}, bf16[288,1024]{1,0:T(8,128)(2,1)}, u32[]{:S(2)}, u32[]{:S(2)}) collective-permute-start(bf16[288,1024]{1,0:T(8,128)(2,1)S(1)} %collective-permute-done.5), channel_id=1, source_target_pairs={{0,4},{4,8},{8,12},{12,16},{16,20},{20,24},{24,28},{28,0},{1,5},{5... | collective-permute-start | bytes 1769480 | tf_op jit(solution)/shard_map/ppermute | solution.py:188
  245.8 111.3 %collective-permute-start.19 = (bf16[3,144,576]{2,1,0:T(8,128)(2,1)S(1)}, bf16[3,144,576]{2,1,0:T(8,128)(2,1)}, u32[]{:S(2)}, u32[]{:S(2)}) collective-permute-start(bf16[3,144,576]{2,1,0:T(8,128)(2,1)S(1)} %bitcast.455), channel_id=1, source_target_pairs={{0,2},{2,0},{1,3},{3,1},{4,6},{6,4},{5,7},{7,5},{8,10},{10,8},{9,1... | collective-permute-start | bytes 1493000 | tf_op jit(solution)/shard_map/ppermute | solution.py:70
  247.4 97.3 %collective-permute-start.20 = (bf16[3,144,576]{2,1,0:T(8,128)(2,1)S(1)}, bf16[3,144,576]{2,1,0:T(8,128)(2,1)}, u32[]{:S(2)}, u32[]{:S(2)}) collective-permute-start(bf16[3,144,576]{2,1,0:T(8,128)(2,1)S(1)} %bitcast.464), channel_id=1, source_target_pairs={{0,4},{4,0},{8,12},{12,8},{16,20},{20,16},{24,28},{28,24},{1,5},{5... | collective-permute-start | bytes 1493000 | tf_op jit(solution)/shard_map/ppermute | solution.py:74
  248.3 108.8 %collective-permute-start.22 = (bf16[3,144,576]{2,1,0:T(8,128)(2,1)}, bf16[3,144,576]{2,1,0:T(8,128)(2,1)}, u32[]{:S(2)}, u32[]{:S(2)}) collective-permute-start(bf16[3,144,576]{2,1,0:T(8,128)(2,1)} %bitcast.436), channel_id=1, source_target_pairs={{0,8},{4,12},{8,0},{12,4},{16,24},{20,28},{24,16},{28,20},{1,9},{5... | collective-permute-start | bytes 1493000 | tf_op jit(solution)/shard_map/ppermute | solution.py:74
  315.2 52.6 %collective-permute-start.24 = (bf16[3,144,576]{2,1,0:T(8,128)(2,1)S(1)}, bf16[3,144,576]{2,1,0:T(8,128)(2,1)}, u32[]{:S(2)}, u32[]{:S(2)}) collective-permute-start(bf16[3,144,576]{2,1,0:T(8,128)(2,1)S(1)} %bitcast.463), channel_id=1, source_target_pairs={{0,12},{4,8},{8,4},{12,0},{16,28},{20,24},{24,20},{28,16},{1,13},{... | collective-permute-start | bytes 1493000 | tf_op jit(solution)/shard_map/ppermute | solution.py:74
  338.3 143.5 %collective-permute-start.18 = (bf16[896,2304]{1,0:T(8,128)(2,1)}, bf16[896,2304]{1,0:T(8,128)(2,1)}, u32[]{:S(2)}, u32[]{:S(2)}) collective-permute-start(bf16[896,2304]{1,0:T(8,128)(2,1)} %get-tuple-element.191), channel_id=1, source_target_pairs={{0,1},{1,0},{2,3},{3,2},{4,5},{5,4},{6,7},{7,6},{8,9},{9,8},{10,11... | collective-permute-start | bytes 12386312 | tf_op jit(solution)/shard_map/ppermute | solution.py:70
  357.1 49.4 %collective-permute-start.26 = (bf16[3,144,576]{2,1,0:T(8,128)(2,1)}, bf16[3,144,576]{2,1,0:T(8,128)(2,1)S(1)}, u32[]{:S(2)}, u32[]{:S(2)}) collective-permute-start(bf16[3,144,576]{2,1,0:T(8,128)(2,1)} %bitcast.468), channel_id=1, source_target_pairs={{0,16},{4,20},{8,24},{12,28},{16,0},{20,4},{24,8},{28,12},{1,17},{... | collective-permute-start | bytes 1493000 | tf_op jit(solution)/shard_map/ppermute | solution.py:74
  357.2 52.4 %collective-permute-start.23 = (bf16[3,144,576]{2,1,0:T(8,128)(2,1)}, bf16[3,144,576]{2,1,0:T(8,128)(2,1)S(1)}, u32[]{:S(2)}, u32[]{:S(2)}) collective-permute-start(bf16[3,144,576]{2,1,0:T(8,128)(2,1)} %collective-permute-done.22), channel_id=1, source_target_pairs={{0,2},{2,0},{1,3},{3,1},{4,6},{6,4},{5,7},{7,5},{8,10},{10,8},{9,1... | collective-permute-start | bytes 1493000 | tf_op jit(solution)/shard_map/ppermute | solution.py:70
  361.9 69.2 %collective-permute-start.28 = (bf16[3,144,576]{2,1,0:T(8,128)(2,1)}, bf16[3,144,576]{2,1,0:T(8,128)(2,1)S(1)}, u32[]{:S(2)}, u32[]{:S(2)}) collective-permute-start(bf16[3,144,576]{2,1,0:T(8,128)(2,1)} %bitcast.467), channel_id=1, source_target_pairs={{0,20},{4,16},{8,28},{12,24},{16,4},{20,0},{24,12},{28,8},{1,21},{... | collective-permute-start | bytes 1493000 | tf_op jit(solution)/shard_map/ppermute | solution.py:74
  367.8 65.8 %collective-permute-start.30 = (bf16[3,144,576]{2,1,0:T(8,128)(2,1)S(1)}, bf16[3,144,576]{2,1,0:T(8,128)(2,1)S(1)}, u32[]{:S(2)}, u32[]{:S(2)}) collective-permute-start(bf16[3,144,576]{2,1,0:T(8,128)(2,1)S(1)} %bitcast.466), channel_id=1, source_target_pairs={{0,24},{4,28},{8,16},{12,20},{16,8},{20,12},{24,0},{28,4},{1,25},{... | collective-permute-start | bytes 1493000 | tf_op jit(solution)/shard_map/ppermute | solution.py:74
  435.6 45.4 %collective-permute-start.33 = (bf16[3,144,576]{2,1,0:T(8,128)(2,1)S(1)}, bf16[3,144,576]{2,1,0:T(8,128)(2,1)S(1)}, u32[]{:S(2)}, u32[]{:S(2)}) collective-permute-start(bf16[3,144,576]{2,1,0:T(8,128)(2,1)S(1)} %collective-permute-done.32), channel_id=1, source_target_pairs={{0,2},{2,0},{1,3},{3,1},{4,6},{6,4},{5,7},{7,5},{8,10},{10,8},{9,1... | collective-permute-start | bytes 1493000 | tf_op jit(solution)/shard_map/ppermute | solution.py:70
  886.8 53.4 %collective-permute-start.67 = (bf16[8,144,576]{2,1,0:T(8,128)(2,1)}, bf16[8,144,576]{2,1,0:T(8,128)(2,1)}, u32[]{:S(2)}, u32[]{:S(2)}) collective-permute-start(bf16[8,144,576]{2,1,0:T(8,128)(2,1)} %fusion.29), channel_id=1, source_target_pairs={{0,2},{2,0},{1,3},{3,1},{4,6},{6,4},{5,7},{7,5},{8,10},{10,8},{9,1... | collective-permute-start | bytes 3981320 | tf_op jit(solution)/shard_map/ppermute | solution.py:70
  897.8 73.2 %collective-permute-start.68 = (bf16[8,144,576]{2,1,0:T(8,128)(2,1)}, bf16[8,144,576]{2,1,0:T(8,128)(2,1)}, u32[]{:S(2)}, u32[]{:S(2)}) collective-permute-start(bf16[8,144,576]{2,1,0:T(8,128)(2,1)} %fusion.30), channel_id=1, source_target_pairs={{0,2},{2,0},{1,3},{3,1},{4,6},{6,4},{5,7},{7,5},{8,10},{10,8},{9,1... | collective-permute-start | bytes 3981320 | tf_op jit(solution)/shard_map/ppermute | solution.py:70
  903.5 72.1 %collective-permute-start.61 = (f32[224,2304]{1,0:T(8,128)}, f32[224,2304]{1,0:T(8,128)}, u32[]{:S(2)}, u32[]{:S(2)}) collective-permute-start(f32[224,2304]{1,0:T(8,128)} %pad_maximum_fusion.4), channel_id=1, source_target_pairs={{0,1},{1,0},{2,3},{3,2},{4,5},{5,4},{6,7},{7,6},{8,9},{9,8},{10,11... | collective-permute-start | bytes 6193160 | tf_op jit(solution)/shard_map/ppermute | solution.py:70
  904.2 74.1 %collective-permute-start.42 = (bf16[112,2304]{1,0:T(8,128)(2,1)}, bf16[112,2304]{1,0:T(8,128)(2,1)S(1)}, u32[]{:S(2)}, u32[]{:S(2)}) collective-permute-start(bf16[112,2304]{1,0:T(8,128)(2,1)} %get-tuple-element.92), channel_id=1, source_target_pairs={{0,1},{1,0},{2,3},{3,2},{4,5},{5,4},{6,7},{7,6},{8,9},{9,8},{10,11... | collective-permute-start | bytes 1548296 | tf_op jit(solution)/shard_map/ppermute | solution.py:70
  980.9 40.9 %collective-permute-start.70 = (bf16[3,144,576]{2,1,0:T(8,128)(2,1)S(1)}, bf16[3,144,576]{2,1,0:T(8,128)(2,1)S(1)}, u32[]{:S(2)}, u32[]{:S(2)}) collective-permute-start(bf16[3,144,576]{2,1,0:T(8,128)(2,1)S(1)} %get-tuple-element.71), channel_id=1, source_target_pairs={{0,8},{4,12},{8,0},{12,4},{16,24},{20,28},{24,16},{28,20},{1,9},{5... | collective-permute-start | bytes 1493000 | tf_op jit(solution)/shard_map/ppermute | solution.py:74
  982.5 51.6 %collective-permute-start.71 = (bf16[3,144,576]{2,1,0:T(8,128)(2,1)S(1)}, bf16[3,144,576]{2,1,0:T(8,128)(2,1)S(1)}, u32[]{:S(2)}, u32[]{:S(2)}) collective-permute-start(bf16[3,144,576]{2,1,0:T(8,128)(2,1)S(1)} %get-tuple-element.70), channel_id=1, source_target_pairs={{0,12},{4,8},{8,4},{12,0},{16,28},{20,24},{24,20},{28,16},{1,13},{... | collective-permute-start | bytes 1493000 | tf_op jit(solution)/shard_map/ppermute | solution.py:74
  983.2 52.9 %collective-permute-start.72 = (bf16[3,144,576]{2,1,0:T(8,128)(2,1)S(1)}, bf16[3,144,576]{2,1,0:T(8,128)(2,1)S(1)}, u32[]{:S(2)}, u32[]{:S(2)}) collective-permute-start(bf16[3,144,576]{2,1,0:T(8,128)(2,1)S(1)} %get-tuple-element.69), channel_id=1, source_target_pairs={{0,16},{4,20},{8,24},{12,28},{16,0},{20,4},{24,8},{28,12},{1,17},{... | collective-permute-start | bytes 1493000 | tf_op jit(solution)/shard_map/ppermute | solution.py:74
  988.9 71.3 %collective-permute-start.73 = (bf16[3,144,576]{2,1,0:T(8,128)(2,1)S(1)}, bf16[3,144,576]{2,1,0:T(8,128)(2,1)S(1)}, u32[]{:S(2)}, u32[]{:S(2)}) collective-permute-start(bf16[3,144,576]{2,1,0:T(8,128)(2,1)S(1)} %get-tuple-element.68), channel_id=1, source_target_pairs={{0,20},{4,16},{8,28},{12,24},{16,4},{20,0},{24,12},{28,8},{1,21},{... | collective-permute-start | bytes 1493000 | tf_op jit(solution)/shard_map/ppermute | solution.py:74
  1001.6 58.6 %collective-permute-start.74 = (bf16[3,144,576]{2,1,0:T(8,128)(2,1)S(1)}, bf16[3,144,576]{2,1,0:T(8,128)(2,1)S(1)}, u32[]{:S(2)}, u32[]{:S(2)}) collective-permute-start(bf16[3,144,576]{2,1,0:T(8,128)(2,1)S(1)} %get-tuple-element.67), channel_id=1, source_target_pairs={{0,24},{4,28},{8,16},{12,20},{16,8},{20,12},{24,0},{28,4},{1,25},{... | collective-permute-start | bytes 1493000 | tf_op jit(solution)/shard_map/ppermute | solution.py:74
  1037.4 138.8 %collective-permute-start.64 = (bf16[224,2304]{1,0:T(8,128)(2,1)}, bf16[224,2304]{1,0:T(8,128)(2,1)}, u32[]{:S(2)}, u32[]{:S(2)}) collective-permute-start(bf16[224,2304]{1,0:T(8,128)(2,1)} %pad_maximum_fusion.7), channel_id=1, source_target_pairs={{0,1},{1,0},{2,3},{3,2},{4,5},{5,4},{6,7},{7,6},{8,9},{9,8},{10,11... | collective-permute-start | bytes 3096584 | tf_op jit(solution)/shard_map/ppermute | solution.py:70
  (147 other events, 2879.4 us)
Sparse Core Ops, SparseCore 0:
  50.0 65.3 all-gather.2
  860.8 150.1 reduce-scatter.3
